TPU v7x, 256 devices: a whole 4x4x8 slice. The times are simulated.
256 devices in a mesh: dp: 16 (over x, y), expert: 16 (over z, core).
Axes of the slice: x: 4, y: 4, z: 8, core: 2. Of those that a mesh axis runs over, the one named last changes fastest.
Arguments:
- hidden_in: bfloat16 [256, 2, 2880], P(('expert', 'dp')), may hold values from -6 to 6
- queries: bfloat16 [256, 2, 4096], P(('expert', 'dp')), may hold values from -2 to 2
- new_keys: bfloat16 [256, 2, 512], P(('expert', 'dp')), may hold values from -2 to 2
- new_values: bfloat16 [256, 2, 512], P(('expert', 'dp')), may hold values from -6 to 6
- key_cache: bfloat16 [256, 512, 512], P(('expert', 'dp')), may hold values from -2 to 2
- value_cache: bfloat16 [256, 512, 512], P(('expert', 'dp')), may hold values from -6 to 6
- prompt_lengths: int32 [256], P(('expert', 'dp')), may hold values from 64 to 512, as said below
- out_weight: bfloat16 [4096, 2880], P('expert'), may hold values from -0.375 to 0.375
- norm_gain: float32 [2880], replicated, may hold values from 0.1 to 1.9
- expert_ids: int32 [256, 2, 4], P('expert'), may hold values from 0 to 31, all different within a row; in each aligned block of 32 rows (0 to 31, 32 to 63, ..., all dimensions but the last counted through in order) at most 12 rows name the same one
- top_logits: bfloat16 [256, 2, 4], P('expert'), may hold values from -4 to 4
- gate_weight: bfloat16 [32, 2880, 2880], P('expert', None, 'dp'), may hold values from -0.109375 to 0.109375
- up_weight: bfloat16 [32, 2880, 2880], P('expert', None, 'dp'), may hold values from -0.109375 to 0.109375
- down_weight: bfloat16 [32, 2880, 2880], P('expert', 'dp'), may hold values from -0.109375 to 0.109375
Outputs:
- layer_out: bfloat16 [256, 2, 2880], P(('expert', 'dp'))
Inputs may be any that keep to these rules, and one draw needn't show every extreme that they name: `prompt_lengths`: some row has exactly 512 live slots. `expert_ids`: A row names 4 different experts at each position. Over the 16 rows held by one index of the expert axis and both positions, no expert is named more than 12 times, and in some such group one expert is named exactly 12 times.
All inputs are finite; a program needn't handle non-finite values.
Results may differ from a plain program's by a relative error of at most 0.02.
Values may be sent and summed in bfloat16 or wider, within the bound.
No kernel may reach another device: no remote copies, remote signals or barrier semaphores. Data moves between devices by JAX's collectives and lax.ppermute only.
A program may use at most 128 MiB of HBM per device.

v0:
```python
import jax
import jax.numpy as jnp
from jax import lax
from jax.sharding import PartitionSpec as P

HQ = 64
KVH = 8
HD = 64


def attend_single(query_rows, fresh_keys, fresh_values, cache_keys, cache_values, length):
    step_count = query_rows.shape[0]
    cache_len = cache_keys.shape[0]
    keys_all = jnp.concatenate([cache_keys, fresh_keys], axis=0).reshape(
        cache_len + step_count, KVH, HD
    )
    values_all = jnp.concatenate([cache_values, fresh_values], axis=0).reshape(
        cache_len + step_count, KVH, HD
    )
    query_heads = query_rows.reshape(step_count, KVH, HQ // KVH, HD)
    scores = (
        jnp.einsum("sgqe,kge->sgqk", query_heads, keys_all, preferred_element_type=jnp.float32)
        * 0.125
    )
    position = jnp.arange(cache_len + step_count, dtype=jnp.int32)
    step_ids = jnp.arange(step_count, dtype=jnp.int32)
    visible = (position[None, :] < length) | (position[None, :] >= cache_len) & (
        position[None, :] - cache_len <= step_ids[:, None]
    )
    exp_scores = jnp.where(visible[:, None, None, :], jnp.exp(scores), jnp.zeros_like(scores))
    attn_probs = (exp_scores / jnp.sum(exp_scores, axis=-1, keepdims=True)).astype(jnp.bfloat16)
    attended = jnp.einsum(
        "sgqk,kge->sgqe", attn_probs, values_all, preferred_element_type=jnp.float32
    )
    return attended.astype(jnp.bfloat16).reshape(step_count, HQ * HD)


def rms_normed(residual, norm_gain):
    inverse_rms = lax.rsqrt(jnp.mean(residual * residual, axis=-1, keepdims=True) + 1e-05)
    return (residual * inverse_rms * norm_gain).astype(jnp.bfloat16)


def swiglu_act(gate_vals, up_vals):
    return (gate_vals * jax.nn.sigmoid(1.702 * gate_vals) * (up_vals + 1.0)).astype(jnp.bfloat16)


def expert_partials(slot_block, gate_weight, up_weight, down_weight):
    results = []
    for local_expert in range(slot_block.shape[1]):
        row_block = slot_block[:, local_expert].reshape(-1, slot_block.shape[3])
        gate_vals = jnp.dot(
            row_block, gate_weight[local_expert], preferred_element_type=jnp.float32
        )
        up_vals = jnp.dot(row_block, up_weight[local_expert], preferred_element_type=jnp.float32)
        activated = swiglu_act(gate_vals, up_vals)
        partial_out = jnp.dot(
            activated, down_weight[local_expert], preferred_element_type=jnp.float32
        )
        results.append(
            partial_out.reshape(slot_block.shape[0], slot_block.shape[2], slot_block.shape[3])
        )
    return jnp.stack(results, axis=1)


def routing_tables(chosen_ids, chosen_logits, experts_all, capacity):
    flat_ids = chosen_ids.reshape(-1, chosen_ids.shape[-1])
    exp_logits = jnp.exp(chosen_logits.reshape(flat_ids.shape).astype(jnp.float32))
    mix_weights = exp_logits / jnp.sum(exp_logits, axis=-1, keepdims=True)
    labels = jnp.arange(experts_all, dtype=jnp.int32)
    match_int = (flat_ids[:, :, None] == labels[None, None, :]).astype(jnp.int32)
    hits_int = jnp.sum(match_int, axis=1)
    slot_int = jnp.cumsum(hits_int, axis=0) - hits_int
    places = jnp.arange(capacity, dtype=jnp.int32)
    select = (
        hits_int.T[:, None, :] * (slot_int.T[:, None, :] == places[None, :, None]).astype(jnp.int32)
    ).astype(jnp.float32)
    token_slots = jnp.take_along_axis(slot_int, flat_ids, axis=1)
    source_rows = flat_ids * capacity + token_slots
    return (select, source_rows, mix_weights)


def gathered_combine(returned_flat, source_rows, mix_weights):
    picked = jnp.take(returned_flat, source_rows.reshape(-1), axis=0)
    picked = picked.reshape(source_rows.shape[0], source_rows.shape[1], returned_flat.shape[1])
    return jnp.sum(picked * mix_weights[:, :, None], axis=1)


def on_device(
    hidden_in,
    queries,
    new_keys,
    new_values,
    key_cache,
    value_cache,
    prompt_lengths,
    out_weight,
    norm_gain,
    expert_ids,
    top_logits,
    gate_weight,
    up_weight,
    down_weight,
):
    row_dev = hidden_in.shape[0]
    step_count = hidden_in.shape[1]
    model_width = hidden_in.shape[2]
    per_index = gate_weight.shape[0]
    expert_group = lax.axis_size("expert")
    experts_all = per_index * expert_group
    attended = jax.vmap(attend_single)(
        queries, new_keys, new_values, key_cache, value_cache, prompt_lengths
    )
    by_heads = lax.all_to_all(attended, "expert", split_axis=2, concat_axis=0, tiled=True)
    projected = lax.psum_scatter(
        jnp.einsum("rsf,fd->rsd", by_heads, out_weight, preferred_element_type=jnp.float32).astype(
            jnp.bfloat16
        ),
        "expert",
        scatter_dimension=0,
        tiled=True,
    ).astype(jnp.float32)
    residual = hidden_in.astype(jnp.float32) + projected
    normed = rms_normed(residual, norm_gain)
    capacity = row_dev * step_count
    start_row = lax.axis_index("dp") * row_dev
    mine_ids = lax.dynamic_slice_in_dim(expert_ids, start_row, row_dev, 0)
    mine_logits = lax.dynamic_slice_in_dim(top_logits, start_row, row_dev, 0)
    select, source_rows, mix_weights = routing_tables(mine_ids, mine_logits, experts_all, capacity)
    dispatch = jnp.einsum(
        "xct,td->xcd",
        select.astype(jnp.bfloat16),
        normed.reshape(-1, model_width),
        preferred_element_type=jnp.float32,
    )
    dispatch = dispatch.astype(jnp.bfloat16).reshape(expert_group, per_index, capacity, model_width)
    arrived = lax.all_to_all(dispatch, "expert", split_axis=0, concat_axis=0, tiled=True)
    partials = expert_partials(
        lax.all_gather(arrived, "dp", axis=0, tiled=True), gate_weight, up_weight, down_weight
    )
    summed = lax.psum_scatter(
        partials.astype(jnp.bfloat16), "dp", scatter_dimension=0, tiled=True
    ).astype(jnp.float32)
    returned = lax.all_to_all(
        summed.astype(jnp.bfloat16), "expert", split_axis=0, concat_axis=0, tiled=True
    ).astype(summed.dtype)
    moe_flat = gathered_combine(
        returned.reshape(experts_all * capacity, model_width), source_rows, mix_weights
    )
    moe_out = moe_flat.reshape(row_dev, step_count, model_width)
    return (residual + moe_out).astype(jnp.bfloat16)


def solution(mesh):
    placed = (
        P(("expert", "dp"), None, None),
        P(("expert", "dp"), None, None),
        P(("expert", "dp"), None, None),
        P(("expert", "dp"), None, None),
        P(("expert", "dp"), None, None),
        P(("expert", "dp"), None, None),
        P(("expert", "dp")),
        P("expert", None),
        P(),
        P("expert", None, None),
        P("expert", None, None),
        P("expert", None, "dp"),
        P("expert", None, "dp"),
        P("expert", "dp", None),
    )
    return jax.shard_map(
        on_device,
        mesh=mesh,
        in_specs=placed,
        out_specs=P(("expert", "dp"), None, None),
        check_vma=False,
    )
```

profile of v0, /device:TPU:1, one launch (start us, length us, event | category | flops | bytes accessed | tf_op | source)
XLA Modules:
  0.0 473.7 jit_solution(13765269799745457546)
XLA Ops:
  7.4 0.8 reshape.325
  8.2 1.1 pad_maximum_fusion.2
  9.3 0.3 copy.81
  9.6 0.3 copy.80
  9.9 0.3 fusion.39
  10.3 0.3 fusion.10
  10.6 0.1 reshape.327
  10.8 3.8 copy.84
  14.6 0.5 broadcast.314
  15.1 23.5 %reduce.9 = bf16[4096,2]{1,0:T(8,128)(2,1)S(1)} reduce(bf16[4096,1,2]{2,1,0:T(2,128)(2,1)} %bitcast.98, bf16[]{:T(256)} %broadcast.314), dimensions={1}, to_apply=%bitcast.89.reduce_sub_computation | reduce | bytes 32770
  38.6 2.2 reshape.367
  40.8 10.0 %all-to-all-start = ((bf16[16,2,256]{2,1,0:T(2,128)(2,1)}), bf16[16,2,256]{2,1,0:T(2,128)(2,1)S(1)}, u32[]{:S(2)}, u32[]{:S(2)}) async-start(bf16[16,2,256]{2,1,0:T(2,128)(2,1)} %reshape.367), calls=%async_computation | async-start | bytes 32768 | tf_op jit(solution)/shard_map/all_to_all | solution.py:113
  50.8 0.2 dynamic-slice_reduce_fusion
  51.0 0.1 convert_reduce_fusion
  51.2 6.9 %all-to-all-done = bf16[16,2,256]{2,1,0:T(2,128)(2,1)S(1)} async-done(((bf16[16,2,256]{2,1,0:T(2,128)(2,1)}), bf16[16,2,256]{2,1,0:T(2,128)(2,1)S(1)}, u32[]{:S(2)}, u32[]{:S(2)}) %all-to-all-start) | async-done | bytes 16416 | tf_op jit(solution)/shard_map/all_to_all | solution.py:113
  58.1 4.3 reshape.368
  62.4 4.6 copy.85
  67.0 0.5 convolution_convert_fusion.3
  67.6 0.8 copy.86
  68.4 0.0 all-gather.2.cloned.1.call-start
  68.5 0.6 dynamic-slice
  69.1 99.8 %all-reduce.5.cloned.1.call-done = bf16[16,2,2880]{2,1,0:T(2,128)(2,1)} async-done(((bf16[16,2,2880]{2,1,0:T(2,128)(2,1)}), bf16[16,2,2880]{2,1,0:T(2,128)(2,1)}) %all-reduce.5.cloned.1.call-update) | async-done | bytes 184336
  168.9 1.4 multiply_reduce_fusion.1
  170.4 1.6 convolution_convert_fusion.2
  172.0 0.3 copy.101
  172.3 20.3 %all_to_all.28 = bf16[16,2,2,2880]{3,2,1,0:T(2,128)(2,1)} all-to-all(bf16[16,2,2,2880]{3,2,1,0:T(2,128)(2,1)S(1)} %bitcast.101), channel_id=1, replica_groups=mesh['dp'=16,'expert'=16] {'expert'}, dimensions={0} | all-to-all | bytes 737280 | tf_op jit(solution)/shard_map/all_to_all | solution.py:136
  192.6 0.2 all-reduce.7.cloned.1.call-start
  192.9 7.0 %fusion.36 = (bf16[1,2880,180]{1,0,2:T(2,128)(2,1)}, bf16[1,2880,180]{1,0,2:T(2,128)(2,1)}) fusion(bf16[2,2880,180]{1,0,2:T(2,128)(2,1)} %param.25), kind=kLoop, calls=%fused_computation.84 | loop fusion | bytes 4147200 | tf_op jit(solution)/shard_map/slice | solution.py:52
  199.9 4.2 fusion.37
  204.1 4.2 fusion.38
  208.3 46.0 %all-gather.2.cloned.1.call-done = bf16[256,2,2,2880]{3,2,1,0:T(2,128)(2,1)} async-done(((bf16[16,2,2,2880]{3,2,1,0:T(2,128)(2,1)}), bf16[256,2,2,2880]{3,2,1,0:T(2,128)(2,1)}) %all-gather.2.cloned.1.call-update) | async-done | bytes 5898256 | tf_op jit(solution)/shard_map/all_gather | solution.py:138
  254.4 8.2 %fusion.35 = (bf16[256,1,2,2880]{3,2,1,0:T(2,128)(2,1)}, bf16[256,1,2,2880]{3,2,1,0:T(2,128)(2,1)}) fusion(bf16[256,2,2,2880]{3,2,1,0:T(2,128)(2,1)} %all-gather.2.cloned.1.call-done), kind=kLoop, calls=%fused_computation.83 | loop fusion | bytes 11796480 | tf_op jit(solution)/shard_map/slice | solution.py:50
  262.6 7.2 %reshape_squeeze.6 = bf16[512,2880]{1,0:T(8,128)(2,1)} reshape(bf16[256,1,2,2880]{3,2,1,0:T(2,128)(2,1)} %get-tuple-element.7) | data formatting | bytes 5898240 | tf_op jit(solution)/shard_map/reshape;squeeze | solution.py:50
  269.7 7.1 %reshape_squeeze.7 = bf16[512,2880]{1,0:T(8,128)(2,1)} reshape(bf16[256,1,2,2880]{3,2,1,0:T(2,128)(2,1)} %get-tuple-element.8) | data formatting | bytes 5898240 | tf_op jit(solution)/shard_map/reshape;squeeze | solution.py:50
  276.9 3.8 fusion.12
  280.7 0.2 copy-done.8
  280.9 1.2 fusion.7
  282.1 0.1 copy.90
  282.2 0.1 reshape.332
  282.4 3.8 fusion.11
  286.3 0.2 copy-done.7
  286.4 1.2 fusion.8
  287.6 0.1 copy.95
  287.8 0.1 reshape.333
  287.9 2.8 fusion
  290.7 1.0 fusion.1
  291.8 3.0 pad_maximum_fusion
  294.8 15.6 %copy.98 = bf16[256,2,2,2880]{3,2,1,0:T(2,128)(2,1)} copy(bf16[256,2,2,2880]{0,3,2,1:T(8,128)(2,1)} %pad_maximum_fusion) | data formatting | bytes 11796480 | tf_op jit(solution)/shard_map/stack | solution.py:62
  310.4 0.1 reshape.336
  310.5 0.6 copy-done.15
  311.1 0.6 dynamic-slice.2
  311.7 0.1 reshape.348
  311.8 0.7 gather_fusion.1
  312.4 0.1 reshape.351
  313.2 0.2 fusion.20
  313.4 127.0 %all-reduce.7.cloned.1.call-done = bf16[256,2,2,2880]{3,2,1,0:T(2,128)(2,1)} async-done(((bf16[256,2,2,2880]{3,2,1,0:T(2,128)(2,1)}), bf16[256,2,2,2880]{3,2,1,0:T(2,128)(2,1)}) %all-reduce.7.cloned.1.call-update) | async-done | bytes 5898256
  440.3 2.0 constant_dynamic-slice_fusion
  442.3 7.7 %all-to-all-start.2 = ((bf16[16,2,2,2880]{3,2,1,0:T(2,128)(2,1)}), bf16[16,2,2,2880]{3,2,1,0:T(2,128)(2,1)S(1)}, u32[]{:S(2)}, u32[]{:S(2)}) async-start(bf16[16,2,2,2880]{3,2,1,0:T(2,128)(2,1)} %constant_dynamic-slice_fusion), calls=%async_computation.2 | async-start | bytes 753664 | tf_op jit(solution)/shard_map/all_to_all | solution.py:143
  450.0 0.1 broadcast_divide_fusion
  450.1 14.1 %all-to-all-done.2 = bf16[16,2,2,2880]{3,2,1,0:T(2,128)(2,1)S(1)} async-done(((bf16[16,2,2,2880]{3,2,1,0:T(2,128)(2,1)}), bf16[16,2,2,2880]{3,2,1,0:T(2,128)(2,1)S(1)}, u32[]{:S(2)}, u32[]{:S(2)}) %all-to-all-start.2) | async-done | bytes 368672 | tf_op jit(solution)/shard_map/all_to_all | solution.py:143
  464.2 0.3 reshape.339
  464.5 0.6 gather_fusion
  465.1 0.1 multiply_reduce_fusion
  465.2 1.9 fusion.17
  (49 shorter events, 0.3 us)
Async XLA Ops:
  6.5 60.5 %copy-start = (bf16[256,2880]{0,1:T(8,128)(2,1)S(1)}, bf16[256,2880]{0,1:T(8,128)(2,1)}, u32[]{:S(2)}) copy-start(bf16[256,2880]{0,1:T(8,128)(2,1)} %param.21) | copy-start | bytes 4423684
  6.5 3.0 copy-start.9
  6.5 3.0 copy-start.13
  15.1 35.7 %copy-start.12 = (s32[16,2,4]{0,2,1:T(4,128)S(1)}, s32[16,2,4]{0,2,1:T(4,128)}, u32[]{:S(2)}) copy-start(s32[16,2,4]{0,2,1:T(4,128)} %param.23) | copy-start | bytes 1540
  40.8 17.3 %all-to-all-start = ((bf16[16,2,256]{2,1,0:T(2,128)(2,1)}), bf16[16,2,256]{2,1,0:T(2,128)(2,1)S(1)}, u32[]{:S(2)}, u32[]{:S(2)}) async-start(bf16[16,2,256]{2,1,0:T(2,128)(2,1)} %reshape.367), calls=%async_computation | async-start | bytes 32768 | tf_op jit(solution)/shard_map/all_to_all | solution.py:113
  50.8 118.2 %all-reduce.5.cloned.1.call-start = ((), (), s32[]{:S(2)}) async-start(), calls=%async_computation.4 | async-start | bytes 376832
  62.4 6.1 %copy-start.16 = (u32[256]{0:T(256)S(1)}, u32[256]{0:T(256)}, u32[]{:S(2)}) copy-start(u32[256]{0:T(256)} %constant.88) | copy-start | bytes 3076
  62.4 106.5 %copy-start.10 = (bf16[1,2,2880]{2,1,0:T(2,128)(2,1)S(1)}, bf16[1,2,2880]{2,1,0:T(2,128)(2,1)}, u32[]{:S(2)}) copy-start(bf16[1,2,2880]{2,1,0:T(2,128)(2,1)} %param.14) | copy-start | bytes 34564
  62.4 107.9 %copy-start.11 = (f32[2880]{0:T(1024)S(1)}, f32[2880]{0:T(1024)}, u32[]{:S(2)}) copy-start(f32[2880]{0:T(1024)} %param.22) | copy-start | bytes 34564
  68.4 185.9 %all-gather.2.cloned.1.call-start = ((), (), s32[]{:S(2)}) async-start(), calls=%async_computation.3 | async-start | bytes 6406144 | tf_op jit(solution)/shard_map/all_gather | solution.py:138
  192.6 247.7 %all-reduce.7.cloned.1.call-start = ((), (), s32[]{:S(2)}) async-start(), calls=%async_computation.5 | async-start | bytes 12058624
  192.9 7.0 %copy-start.2 = (bf16[2,2880,180]{1,0,2:T(2,128)(2,1)S(1)}, bf16[2,2880,180]{1,0,2:T(2,128)(2,1)}, u32[]{:S(2)}) copy-start(bf16[2,2880,180]{1,0,2:T(2,128)(2,1)} %param.26) | copy-start | bytes 6220804
  199.9 4.2 copy-start.3
  276.9 3.8 copy-start.6
  276.9 4.0 copy-start.8
  282.4 3.9 copy-start.5
  282.4 4.0 copy-start.7
  287.9 2.8 copy-start.4
  310.4 0.7 copy-start.15
  310.4 2.8 copy-start.14
  311.8 155.4 %copy-start.1 = (bf16[256,2880]{0,1:T(8,128)(2,1)S(1)}, bf16[256,2880]{0,1:T(8,128)(2,1)}, u32[]{:S(2)}) copy-start(bf16[256,2880]{0,1:T(8,128)(2,1)} %param.21) | copy-start | bytes 4423684
  442.3 21.9 %all-to-all-start.2 = ((bf16[16,2,2,2880]{3,2,1,0:T(2,128)(2,1)}), bf16[16,2,2,2880]{3,2,1,0:T(2,128)(2,1)S(1)}, u32[]{:S(2)}, u32[]{:S(2)}) async-start(bf16[16,2,2,2880]{3,2,1,0:T(2,128)(2,1)} %constant_dynamic-slice_fusion), calls=%async_computation.2 | async-start | bytes 753664 | tf_op jit(solution)/shard_map/all_to_all | solution.py:143
Sparse Core Ops, SparseCore 0:
  68.6 100.3 all-reduce.4
  192.8 61.5 all-gather.1
  310.6 129.7 all-reduce.6
where the time goes:
time: 475 us; the launch traced here: 474 us
  waiting for transfers between devices  294 us (62%)
  local copies, waits for them, and re-layouts  78.4 us (17%)
  other arithmetic  31.5 us (7%)
  blocking collectives  20.3 us (4%)
  starting transfers between devices  18 us (4%)
  matrix products  16.7 us (4%)
  between operations  14.9 us (3%)
    unnamed x5, waiting for transfers between devices  227 us
    all_gather x1, waiting for transfers between devices, on_device(): lax.all_gather(arrived, 'dp', axis=0, tiled=True)  46 us
    unnamed x1, other arithmetic  23.5 us
    all_to_all x1, blocking collectives, on_device(): lax.all_to_all(dispatch, 'expert', split_axis=0, concat_axis=0, tiled=True)  20.3 us
    another operation x1, local copies, waits for them, and re-layouts, expert_partials(): return jnp.stack(results, axis=1)  15.6 us
    another operation x2, local copies, waits for them, and re-layouts, expert_partials(): row_block = slot_block[:, local_expert].reshape(-1, slot_block.shape[3])  14.3 us
    all_to_all x1, waiting for transfers between devices, on_device(): lax.all_to_all(summed.astype(jnp.bfloat16), 'expert', split_axis=0, conca...  14.1 us
    unnamed x40, local copies, waits for them, and re-layouts  11.2 us
  transfers between devices with their start and end apart: 5, of which 5 were waited for; matrix products, arithmetic and copies ran while one was open for 4% of the time, Pallas kernels for 0%

commit v1 on v0

--- a/solution.py
+++ b/solution.py
@@ -110,7 +110,12 @@
     attended = jax.vmap(attend_single)(
         queries, new_keys, new_values, key_cache, value_cache, prompt_lengths
     )
-    by_heads = lax.all_to_all(attended, "expert", split_axis=2, concat_axis=0, tiled=True)
+    by_heads = jnp.concatenate(
+        lax.all_to_all(
+            jnp.stack(jnp.split(attended, lax.axis_size("expert"), axis=2)), "expert", 0, 0
+        ),
+        axis=0,
+    )
     projected = lax.psum_scatter(
         jnp.einsum("rsf,fd->rsd", by_heads, out_weight, preferred_element_type=jnp.float32).astype(
             jnp.bfloat16

time: 475 us -> 445 us (0.937)
  other arithmetic: 31.5 us -> 8.18 us
  local copies, waits for them, and re-layouts: 78.4 us -> 72.1 us
    unnamed x1 -> x0, other arithmetic: 23.5 us -> none
    unnamed x40 -> x52, local copies, waits for them, and re-layouts: 11.2 us -> 12.7 us
where the time goes in v1:
time: 445 us; the launch traced here: 444 us
  waiting for transfers between devices  294 us (66%)
  local copies, waits for them, and re-layouts  72.1 us (16%)
  blocking collectives  20.3 us (5%)
  starting transfers between devices  18 us (4%)
  matrix products  16.7 us (4%)
  between operations  14.9 us (3%)
  other arithmetic  8.18 us (2%)
    unnamed x5, waiting for transfers between devices  227 us
    all_gather x1, waiting for transfers between devices, on_device(): lax.all_gather(arrived, 'dp', axis=0, tiled=True)  45.9 us
    all_to_all x1, blocking collectives, on_device(): lax.all_to_all(dispatch, 'expert', split_axis=0, concat_axis=0, tiled=True)  20.3 us
    another operation x1, local copies, waits for them, and re-layouts, expert_partials(): return jnp.stack(results, axis=1)  15.6 us
    another operation x2, local copies, waits for them, and re-layouts, expert_partials(): row_block = slot_block[:, local_expert].reshape(-1, slot_block.shape[3])  14.3 us
    all_to_all x1, waiting for transfers between devices, on_device(): lax.all_to_all(summed.astype(jnp.bfloat16), 'expert', split_axis=0, conca...  14.1 us
    unnamed x52, local copies, waits for them, and re-layouts  12.7 us
    all_to_all x1, starting transfers between devices, on_device(): lax.all_to_all(jnp.stack(jnp.split(attended, lax.axis_size('expert'), axi...  9.98 us
  transfers between devices with their start and end apart: 5, of which 5 were waited for; matrix products, arithmetic and copies ran while one was open for 4% of the time, Pallas kernels for 0%

profile of v1, /device:TPU:1, one launch (start us, length us, event | category | flops | bytes accessed | tf_op | source)
XLA Modules:
  0.0 443.9 jit_solution(9646688929630829948)
XLA Ops:
  7.4 0.8 reshape.328
  8.2 1.1 pad_maximum_fusion.2
  9.3 0.3 copy.129
  9.6 0.3 copy.128
  10.0 0.3 fusion.40
  10.3 0.3 fusion.10
  10.8 0.6 constant_dynamic-update-slice_fusion.15
  11.4 0.6 constant_dynamic-update-slice_fusion.14
  12.0 0.6 constant_dynamic-update-slice_fusion.13
  12.5 0.5 constant_dynamic-update-slice_fusion.12
  13.1 0.5 constant_dynamic-update-slice_fusion.11
  13.6 0.6 constant_dynamic-update-slice_fusion.10
  14.2 0.6 constant_dynamic-update-slice_fusion.9
  14.8 0.6 constant_dynamic-update-slice_fusion.8
  15.4 0.6 constant_dynamic-update-slice_fusion.7
  15.9 0.5 constant_dynamic-update-slice_fusion.6
  16.5 0.6 constant_dynamic-update-slice_fusion.5
  17.0 0.6 constant_dynamic-update-slice_fusion.4
  17.6 0.5 constant_dynamic-update-slice_fusion.3
  18.2 0.6 constant_dynamic-update-slice_fusion.2
  18.8 0.6 constant_dynamic-update-slice_fusion.1
  19.3 0.6 constant_dynamic-update-slice_fusion
  19.9 10.0 %all-to-all-start = ((bf16[16,1,2,256]{3,2,1,0:T(2,128)(2,1)}), bf16[16,1,2,256]{3,2,1,0:T(2,128)(2,1)S(1)}, u32[]{:S(2)}, u32[]{:S(2)}) async-start(bf16[16,1,2,256]{3,2,1,0:T(2,128)(2,1)} %constant_dynamic-update-slice_fusion), calls=%async_computation | async-start | bytes 32768 | tf_op jit(solution)/shard_map/all_to_all | solution.py:114
  30.0 0.2 dynamic-slice_reduce_fusion
  30.3 6.9 %all-to-all-done = bf16[16,1,2,256]{3,2,1,0:T(2,128)(2,1)S(1)} async-done(((bf16[16,1,2,256]{3,2,1,0:T(2,128)(2,1)}), bf16[16,1,2,256]{3,2,1,0:T(2,128)(2,1)S(1)}, u32[]{:S(2)}, u32[]{:S(2)}) %all-to-all-start) | async-done | bytes 16416 | tf_op jit(solution)/shard_map/all_to_all | solution.py:114
  37.3 0.5 convolution_convert_fusion.3
  37.8 0.8 copy.133
  38.7 0.6 dynamic-slice
  39.3 99.6 %all-reduce.5.cloned.1.call-done = bf16[16,2,2880]{2,1,0:T(2,128)(2,1)} async-done(((bf16[16,2,2880]{2,1,0:T(2,128)(2,1)}), bf16[16,2,2880]{2,1,0:T(2,128)(2,1)}) %all-reduce.5.cloned.1.call-update) | async-done | bytes 184336
  139.0 1.5 multiply_reduce_fusion.1
  140.4 1.7 convolution_convert_fusion.2
  142.1 0.3 copy.148
  142.4 20.3 %all_to_all.15 = bf16[16,2,2,2880]{3,2,1,0:T(2,128)(2,1)} all-to-all(bf16[16,2,2,2880]{3,2,1,0:T(2,128)(2,1)S(1)} %bitcast.153), channel_id=1, replica_groups=mesh['dp'=16,'expert'=16] {'expert'}, dimensions={0} | all-to-all | bytes 737280 | tf_op jit(solution)/shard_map/all_to_all | solution.py:141
  162.8 0.2 all-reduce.7.cloned.1.call-start
  163.0 7.1 %fusion.37 = (bf16[1,2880,180]{1,0,2:T(2,128)(2,1)}, bf16[1,2880,180]{1,0,2:T(2,128)(2,1)}) fusion(bf16[2,2880,180]{1,0,2:T(2,128)(2,1)} %param.25), kind=kLoop, calls=%fused_computation.116 | loop fusion | bytes 4147200 | tf_op jit(solution)/shard_map/slice | solution.py:52
  170.1 4.2 fusion.38
  174.3 4.2 fusion.39
  178.5 45.9 %all-gather.2.cloned.1.call-done = bf16[256,2,2,2880]{3,2,1,0:T(2,128)(2,1)} async-done(((bf16[16,2,2,2880]{3,2,1,0:T(2,128)(2,1)}), bf16[256,2,2,2880]{3,2,1,0:T(2,128)(2,1)}) %all-gather.2.cloned.1.call-update) | async-done | bytes 5898256 | tf_op jit(solution)/shard_map/all_gather | solution.py:143
  224.5 8.2 %fusion.36 = (bf16[256,1,2,2880]{3,2,1,0:T(2,128)(2,1)}, bf16[256,1,2,2880]{3,2,1,0:T(2,128)(2,1)}) fusion(bf16[256,2,2,2880]{3,2,1,0:T(2,128)(2,1)} %all-gather.2.cloned.1.call-done), kind=kLoop, calls=%fused_computation.115 | loop fusion | bytes 11796480 | tf_op jit(solution)/shard_map/slice | solution.py:50
  232.7 7.1 %reshape_squeeze.6 = bf16[512,2880]{1,0:T(8,128)(2,1)} reshape(bf16[256,1,2,2880]{3,2,1,0:T(2,128)(2,1)} %get-tuple-element.7) | data formatting | bytes 5898240 | tf_op jit(solution)/shard_map/reshape;squeeze | solution.py:50
  239.8 7.2 %reshape_squeeze.7 = bf16[512,2880]{1,0:T(8,128)(2,1)} reshape(bf16[256,1,2,2880]{3,2,1,0:T(2,128)(2,1)} %get-tuple-element.8) | data formatting | bytes 5898240 | tf_op jit(solution)/shard_map/reshape;squeeze | solution.py:50
  247.0 3.8 fusion.12
  250.8 0.2 copy-done.8
  251.0 1.2 fusion.7
  252.4 0.1 reshape.336
  252.5 3.8 fusion.11
  256.4 0.2 copy-done.7
  256.6 1.2 fusion.8
  258.1 2.8 fusion
  260.9 1.0 fusion.1
  261.9 3.0 pad_maximum_fusion
  265.0 15.6 %copy.145 = bf16[256,2,2,2880]{3,2,1,0:T(2,128)(2,1)} copy(bf16[256,2,2,2880]{0,3,2,1:T(8,128)(2,1)} %pad_maximum_fusion) | data formatting | bytes 11796480 | tf_op jit(solution)/shard_map/stack | solution.py:62
  280.7 0.6 copy-done.15
  281.2 0.6 dynamic-slice.2
  281.9 0.7 gather_fusion.1
  283.3 0.2 fusion.21
  283.5 127.0 %all-reduce.7.cloned.1.call-done = bf16[256,2,2,2880]{3,2,1,0:T(2,128)(2,1)} async-done(((bf16[256,2,2,2880]{3,2,1,0:T(2,128)(2,1)}), bf16[256,2,2,2880]{3,2,1,0:T(2,128)(2,1)}) %all-reduce.7.cloned.1.call-update) | async-done | bytes 5898256
  410.5 2.0 constant_dynamic-slice_fusion
  412.5 7.7 %all-to-all-start.2 = ((bf16[16,2,2,2880]{3,2,1,0:T(2,128)(2,1)}), bf16[16,2,2,2880]{3,2,1,0:T(2,128)(2,1)S(1)}, u32[]{:S(2)}, u32[]{:S(2)}) async-start(bf16[16,2,2,2880]{3,2,1,0:T(2,128)(2,1)} %constant_dynamic-slice_fusion), calls=%async_computation.2 | async-start | bytes 753664 | tf_op jit(solution)/shard_map/all_to_all | solution.py:148
  420.3 14.1 %all-to-all-done.2 = bf16[16,2,2,2880]{3,2,1,0:T(2,128)(2,1)S(1)} async-done(((bf16[16,2,2,2880]{3,2,1,0:T(2,128)(2,1)}), bf16[16,2,2,2880]{3,2,1,0:T(2,128)(2,1)S(1)}, u32[]{:S(2)}, u32[]{:S(2)}) %all-to-all-start.2) | async-done | bytes 368672 | tf_op jit(solution)/shard_map/all_to_all | solution.py:148
  434.4 0.3 reshape.343
  434.7 0.6 gather_fusion
  435.3 0.1 multiply_reduce_fusion
  435.5 1.9 fusion.17
  (59 shorter events, 1.3 us)
Async XLA Ops:
  6.5 30.7 %copy-start = (bf16[256,2880]{0,1:T(8,128)(2,1)S(1)}, bf16[256,2880]{0,1:T(8,128)(2,1)}, u32[]{:S(2)}) copy-start(bf16[256,2880]{0,1:T(8,128)(2,1)} %param.21) | copy-start | bytes 4423684
  6.5 3.0 copy-start.9
  6.5 3.0 copy-start.13
  9.6 20.3 %copy-start.12 = (s32[16,2,4]{0,2,1:T(4,128)S(1)}, s32[16,2,4]{0,2,1:T(4,128)}, u32[]{:S(2)}) copy-start(s32[16,2,4]{0,2,1:T(4,128)} %param.23) | copy-start | bytes 1540
  10.3 28.5 %copy-start.16 = (u32[256]{0:T(256)S(1)}, u32[256]{0:T(256)}, u32[]{:S(2)}) copy-start(u32[256]{0:T(256)} %constant.88) | copy-start | bytes 3076
  10.3 128.7 %copy-start.10 = (bf16[1,2,2880]{2,1,0:T(2,128)(2,1)S(1)}, bf16[1,2,2880]{2,1,0:T(2,128)(2,1)}, u32[]{:S(2)}) copy-start(bf16[1,2,2880]{2,1,0:T(2,128)(2,1)} %param.14) | copy-start | bytes 34564
  10.3 130.2 %copy-start.11 = (f32[2880]{0:T(1024)S(1)}, f32[2880]{0:T(1024)}, u32[]{:S(2)}) copy-start(f32[2880]{0:T(1024)} %param.22) | copy-start | bytes 34564
  19.9 17.3 %all-to-all-start = ((bf16[16,1,2,256]{3,2,1,0:T(2,128)(2,1)}), bf16[16,1,2,256]{3,2,1,0:T(2,128)(2,1)S(1)}, u32[]{:S(2)}, u32[]{:S(2)}) async-start(bf16[16,1,2,256]{3,2,1,0:T(2,128)(2,1)} %constant_dynamic-update-slice_fusion), calls=%async_computation | async-start | bytes 32768 | tf_op jit(solution)/shard_map/all_to_all | solution.py:114
  29.9 109.0 %all-reduce.5.cloned.1.call-start = ((), (), s32[]{:S(2)}) async-start(), calls=%async_computation.4 | async-start | bytes 376832
  38.7 185.8 %all-gather.2.cloned.1.call-start = ((), (), s32[]{:S(2)}) async-start(), calls=%async_computation.3 | async-start | bytes 6406144 | tf_op jit(solution)/shard_map/all_gather | solution.py:143
  162.8 247.8 %all-reduce.7.cloned.1.call-start = ((), (), s32[]{:S(2)}) async-start(), calls=%async_computation.5 | async-start | bytes 12058624
  163.0 7.1 %copy-start.2 = (bf16[2,2880,180]{1,0,2:T(2,128)(2,1)S(1)}, bf16[2,2880,180]{1,0,2:T(2,128)(2,1)}, u32[]{:S(2)}) copy-start(bf16[2,2880,180]{1,0,2:T(2,128)(2,1)} %param.26) | copy-start | bytes 6220804
  170.1 4.2 copy-start.3
  247.0 3.8 copy-start.6
  247.0 4.0 copy-start.8
  252.5 3.9 copy-start.5
  252.5 4.0 copy-start.7
  258.1 2.8 copy-start.4
  280.6 0.7 copy-start.15
  280.6 2.8 copy-start.14
  281.9 155.5 %copy-start.1 = (bf16[256,2880]{0,1:T(8,128)(2,1)S(1)}, bf16[256,2880]{0,1:T(8,128)(2,1)}, u32[]{:S(2)}) copy-start(bf16[256,2880]{0,1:T(8,128)(2,1)} %param.21) | copy-start | bytes 4423684
  412.5 21.9 %all-to-all-start.2 = ((bf16[16,2,2,2880]{3,2,1,0:T(2,128)(2,1)}), bf16[16,2,2,2880]{3,2,1,0:T(2,128)(2,1)S(1)}, u32[]{:S(2)}, u32[]{:S(2)}) async-start(bf16[16,2,2,2880]{3,2,1,0:T(2,128)(2,1)} %constant_dynamic-slice_fusion), calls=%async_computation.2 | async-start | bytes 753664 | tf_op jit(solution)/shard_map/all_to_all | solution.py:148
Sparse Core Ops, SparseCore 0:
  38.8 100.1 all-reduce.4
  162.9 61.5 all-gather.1
  280.7 129.7 all-reduce.6
